TPU v7x, 256 devices: a whole 4x4x8 slice. The times are simulated.
256 devices in a mesh: seq: 64 (over x, z, core), head: 4 (over y).
Axes of the slice: x: 4, y: 4, z: 8, core: 2. Of those that a mesh axis runs over, the one named last changes fastest.
Arguments:
- frames: bfloat16 [16384, 1024], P('seq'), may hold values from -6 to 6
- norm_gain: float32 [1024], replicated, may hold values from 0.5 to 1.5
- w_qkv: bfloat16 [3, 1024, 1024], P(None, None, 'head'), may hold values from -2 to 2
- w_out: bfloat16 [1024, 1024], P('head'), may hold values from -0.1875 to 0.1875
- w_proj: bfloat16 [1024, 512], replicated, may hold values from -0.1875 to 0.1875
- text_table: bfloat16 [32768, 512], P(('seq', 'head')), may hold values from -6 to 6
- token_ids: int32 [512, 16], replicated, may hold values from 0 to 32767
- span_bounds: int32 [512, 2], P(('seq', 'head')), may hold values from 0 to 16384, as said below
- contrast_divisor: float32 [1], replicated, may hold values from 10 to 30
Outputs:
- interval_embedding_derivative: float32 [512, 512], P(('seq', 'head'))
- loss_terms: float32 [512], P(('seq', 'head'))
Inputs may be any that keep to these rules, and one draw needn't show every extreme that they name: `span_bounds`: both entries are multiples of 128 and the first is smaller than the second.
All inputs are finite; a program needn't handle non-finite values.
Results may differ from a plain program's by a relative error of at most 0.006.
Values may be sent and summed in bfloat16 or wider, within the bound.
A program may use at most 64 MiB of HBM per device.

v0:
```python
import jax
import jax.numpy as jnp
from jax import lax
from jax.sharding import PartitionSpec as P

HDIM = 64
E = 512
BLK = 128


def extended(cells, sides, width):
    for axis, dim in sides:
        count = lax.axis_size(axis)
        ends = count - 1
        head = lax.slice_in_dim(cells, 0, width, axis=dim)
        tail = lax.slice_in_dim(cells, cells.shape[dim] - width, cells.shape[dim], axis=dim)
        cells = jnp.concatenate(
            [
                lax.ppermute(tail, axis, [(i, (i + 1) % count) for i in range(ends)]),
                cells,
                lax.ppermute(head, axis, [((i + 1) % count, i) for i in range(ends)]),
            ],
            axis=dim,
        )
    return cells


def log_total(values, axis):
    return jnp.log(jnp.sum(jnp.exp(values), axis=axis))


def unit_rows(values):
    return (
        values * lax.rsqrt(jnp.mean(values * values, axis=-1, keepdims=True) + 1e-06) * E ** (-0.5)
    )


def token_counts(chosen, vocab_ids):

    def add_token(position, counts):
        column = lax.dynamic_index_in_dim(chosen, position, 1, keepdims=False)
        return counts + (column[:, None] == vocab_ids[None, :]).astype(jnp.float32)

    return lax.fori_loop(
        0, chosen.shape[1], add_token, jnp.zeros((chosen.shape[0], vocab_ids.shape[0]), jnp.float32)
    )


def local(
    frames, norm_gain, w_qkv, w_out, w_proj, text_table, token_ids, span_bounds, contrast_divisor
):
    frame_rows = frames.shape[0]
    head_cols = w_qkv.shape[2]
    local_heads = head_cols // HDIM
    seq_count = lax.axis_size("seq")
    total_frames = frame_rows * seq_count
    first_frame = lax.axis_index("seq") * frame_rows
    as32 = frames.astype(jnp.float32)
    normed = (
        as32 * lax.rsqrt(jnp.mean(as32 * as32, axis=-1, keepdims=True) + 1e-05) * norm_gain
    ).astype(jnp.bfloat16)
    queries = jnp.dot(normed, w_qkv[0], preferred_element_type=jnp.float32).astype(jnp.bfloat16)
    keys_now = jnp.dot(normed, w_qkv[1], preferred_element_type=jnp.float32).astype(jnp.bfloat16)
    values_now = jnp.dot(normed, w_qkv[2], preferred_element_type=jnp.float32).astype(jnp.bfloat16)
    pairs = jnp.concatenate([keys_now, values_now], axis=1)
    padded = extended(pairs, (("seq", 0),), frame_rows)
    query_block = min(512, frame_rows)
    span_width = 2 * frame_rows + query_block

    def attend(block):
        begin = block * query_block
        query_part = queries.reshape(query_block, local_heads, HDIM)
        key_part = padded[:, :head_cols].reshape(span_width, local_heads, HDIM)
        value_part = padded[:, head_cols:].reshape(span_width, local_heads, HDIM)
        scores = jnp.einsum(
            "qhd,khd->hqk", query_part, key_part, preferred_element_type=jnp.float32
        ) * HDIM ** (-0.5)
        query_pos = first_frame + begin + jnp.arange(query_block, dtype=jnp.int32)
        key_pos = first_frame + begin - frame_rows + jnp.arange(span_width, dtype=jnp.int32)
        allowed = (
            (jnp.abs(query_pos[:, None] - key_pos[None, :]) <= frame_rows)
            & (key_pos >= 0)[None, :]
            & (key_pos < total_frames)[None, :]
        )
        scores = jnp.where(allowed[None], scores, -1e30)
        top = jnp.max(scores, axis=2, keepdims=True)
        probs = jnp.exp(scores - top)
        denom = jnp.sum(probs, axis=2)
        mixed = jnp.einsum(
            "hqk,khd->qhd",
            probs.astype(jnp.bfloat16),
            value_part,
            preferred_element_type=jnp.float32,
        )
        return (mixed / denom.T[:, :, None]).astype(jnp.bfloat16).reshape(query_block, head_cols)

    attended = lax.map(attend, jnp.arange(frame_rows // query_block, dtype=jnp.int32)).reshape(
        frame_rows, head_cols
    )
    block_count = frame_rows // BLK
    out_sums = attended.astype(jnp.float32).reshape(block_count, BLK, head_cols).sum(axis=1)
    head_slot = lax.axis_index("head")
    own_features = lax.dynamic_slice_in_dim(as32, head_slot * head_cols, head_cols, 1)
    feature_sums = own_features.reshape(block_count, BLK, head_cols).sum(axis=1)
    proj_rows = lax.dynamic_slice_in_dim(w_proj, head_slot * head_cols, head_cols, 0)
    through_out = jnp.dot(out_sums, w_out.astype(jnp.float32), precision=lax.Precision.HIGHEST)
    partial_value = jnp.dot(
        through_out, w_proj.astype(jnp.float32), precision=lax.Precision.HIGHEST
    ) + jnp.dot(feature_sums, proj_rows.astype(jnp.float32), precision=lax.Precision.HIGHEST)
    everyone = lax.all_gather(partial_value, ("seq", "head"), axis=0, tiled=True)
    head_count = lax.axis_size("head")
    block_table = (
        everyone.reshape(seq_count, head_count, block_count, -1)
        .sum(axis=1)
        .reshape(seq_count * block_count, -1)
    )
    total_blocks = block_table.shape[0]
    block_ids = jnp.arange(total_blocks, dtype=jnp.int32)
    lower = span_bounds[:, 0] // BLK
    upper = span_bounds[:, 1] // BLK
    span_mask = (
        (block_ids[None, :] >= lower[:, None]) & (block_ids[None, :] < upper[:, None])
    ).astype(jnp.float32)
    pooled = jnp.dot(span_mask, block_table, precision=lax.Precision.HIGHEST)
    interval_embedding_rows = unit_rows(pooled).astype(jnp.bfloat16)
    own_caps = span_bounds.shape[0]
    all_caps = token_ids.shape[0]
    slot = lax.axis_index(("seq", "head"))
    first_caption = slot * own_caps
    vocab_rows = text_table.shape[0]
    vocab_ids = slot * vocab_rows + jnp.arange(vocab_rows, dtype=jnp.int32)
    counts = token_counts(token_ids, vocab_ids)
    raw = lax.psum_scatter(
        jnp.dot(counts.astype(jnp.bfloat16), text_table, preferred_element_type=jnp.float32),
        ("seq", "head"),
        scatter_dimension=0,
        tiled=True,
    )
    caption_own = unit_rows(raw).astype(jnp.bfloat16)
    spans_all, captions_all = (
        lax.all_gather(interval_embedding_rows, ("seq", "head"), axis=0, tiled=True),
        lax.all_gather(caption_own, ("seq", "head"), axis=0, tiled=True),
    )
    normalizer_divisor = contrast_divisor[0]
    row_logits = (
        jnp.einsum("je,ie->ji", caption_own, spans_all, preferred_element_type=jnp.float32)
        * normalizer_divisor
    )
    col_logits = (
        jnp.einsum(
            "je,ie->ji", captions_all, interval_embedding_rows, preferred_element_type=jnp.float32
        )
        * normalizer_divisor
    )
    row_total = log_total(row_logits, 1)
    col_total = log_total(col_logits, 0)
    own_square = lax.dynamic_slice_in_dim(row_logits, first_caption, own_caps, 1)
    loss_terms = 0.5 * (row_total + col_total) - jnp.diagonal(own_square)
    row_totals = lax.all_gather(row_total, ("seq", "head"), axis=0, tiled=True)
    marker = (
        jnp.arange(all_caps, dtype=jnp.int32)[:, None]
        == first_caption + jnp.arange(own_caps, dtype=jnp.int32)[None, :]
    ).astype(jnp.float32)
    derivative_multipliers = (
        0.5 * jnp.exp(col_logits - row_totals[:, None])
        + 0.5 * jnp.exp(col_logits - col_total[None, :])
        - marker
    ).astype(jnp.bfloat16)
    interval_embedding_derivative = (
        jnp.einsum(
            "ji,je->ie", derivative_multipliers, captions_all, preferred_element_type=jnp.float32
        )
        * normalizer_divisor
    )
    return (interval_embedding_derivative, loss_terms)


def solution(mesh):
    placed = (
        P("seq", None),
        P(),
        P(None, None, "head"),
        P("head", None),
        P(),
        P(("seq", "head"), None),
        P(),
        P(("seq", "head"), None),
        P(),
    )
    return jax.shard_map(
        local,
        mesh=mesh,
        in_specs=placed,
        out_specs=(P(("seq", "head"), None), P(("seq", "head"))),
        check_vma=False,
    )
```

profile of v0, /device:TPU:1, one launch (start us, length us, event | category | flops | bytes accessed | tf_op | source)
XLA Modules:
  0.0 622.0 jit_solution(1436011307544993010)
XLA Ops:
  7.2 1.3 multiply_reduce_fusion
  8.5 1.7 convolution_convert_fusion.1
  10.3 1.7 convolution_convert_fusion.2
  12.0 5.1 collective-permute-start
  17.0 2.2 collective-permute-start.1
  19.2 14.5 %while.18 = (s32[]{:T(128)}, f32[512,128]{1,0:T(8,128)S(1)}, s32[512,16]{0,1:T(8,128)}, s32[]{:T(128)}, s32[]{:T(128)}, /*index=5*/s32[]{:T(128)}) while((s32[]{:T(128)}, f32[512,128]{1,0:T(8,128)S(1)}, s32[512,16]{0,1:T(8,128)}, s32[]{:T(128)}, s32[]{:T(128)}, /*index=5*/s32[]{:T(128)}) %tuple.47), condition=%wide.region_1.2_spmd.clone, body=%wide.region_0.0_spmd.clone.sunk | while | flops 262275 | bytes 531543 | solution.py:44
  19.2 0.7 constant_dynamic-slice_fusion.4
  20.2 0.7 constant_dynamic-slice_fusion.4
  21.1 0.7 constant_dynamic-slice_fusion.4
  22.0 0.7 constant_dynamic-slice_fusion.4
  22.9 0.7 constant_dynamic-slice_fusion.4
  23.8 0.7 constant_dynamic-slice_fusion.4
  24.7 0.7 constant_dynamic-slice_fusion.4
  25.6 0.7 constant_dynamic-slice_fusion.4
  26.5 0.7 constant_dynamic-slice_fusion.4
  27.4 0.7 constant_dynamic-slice_fusion.4
  33.7 1.3 fusion.30
  35.7 1.5 convolution_convert_fusion
  37.2 1.1 pad_maximum_fusion
  38.4 0.8 fusion.2
  39.2 0.9 fusion.3
  40.1 1.0 fusion.18
  42.5 0.8 fusion.11
  44.4 251.9 %all-reduce.4.cloned.1.call-done = f32[512,512]{1,0:T(8,128)} async-done(((f32[512,512]{1,0:T(8,128)}), f32[512,512]{1,0:T(8,128)}) %all-reduce.4.cloned.1.call-update) | async-done | bytes 1048592
  296.3 0.8 multiply_reduce_fusion.2
  297.1 0.8 fusion.74
  297.9 118.1 %all-gather = bf16[256,2,512]{2,1,0:T(2,128)(2,1)S(1)} all-gather(bf16[1,2,512]{2,1,0:T(2,128)(2,1)S(1)} %fusion.74), channel_id=1, replica_groups=mesh['seq'=64,'head'=4] {'seq','head'}, dimensions={0}, use_global_device_ids=true | all-gather | bytes 526336 | tf_op jit(solution)/shard_map/all_gather | solution.py:142
  416.3 1.8 bitcast_reduce_fusion
  418.7 116.9 %all-gather.2 = bf16[256,2,512]{2,1,0:T(2,128)(2,1)S(1)} all-gather(bf16[1,2,512]{2,1,0:T(2,128)(2,1)S(1)} %fusion.73), channel_id=1, replica_groups=mesh['seq'=64,'head'=4] {'seq','head'}, dimensions={0}, use_global_device_ids=true | all-gather | bytes 526336 | tf_op jit(solution)/shard_map/all_gather | solution.py:141
  535.8 1.1 exponential_reduce_fusion.1
  538.5 75.9 %all-reduce = f32[512]{0:T(512)S(1)} all-reduce(f32[512]{0:T(512)S(1)} %get-tuple-element.129), channel_id=1, replica_groups=mesh['seq'=64,'head'=4] {'seq','head'}, use_global_device_ids=true, to_apply=%add | all-reduce | flops 512 | bytes 4096
  614.4 0.8 convolution_multiply_fusion
  (86 shorter events, 11.9 us)
Async XLA Ops:
  7.2 34.9 %copy-start = (bf16[1024,512]{1,0:T(8,128)(2,1)S(1)}, bf16[1024,512]{1,0:T(8,128)(2,1)}, u32[]{:S(2)}) copy-start(bf16[1024,512]{1,0:T(8,128)(2,1)} %param.15) | copy-start | bytes 3145732
  7.2 289.1 %all-reduce.4.cloned.1.call-start = ((), (), s32[]{:S(2)}) async-start(), calls=%async_computation.1 | async-start | bytes 2097152
  8.5 25.2 %copy-start.3 = (bf16[128,512]{1,0:T(8,128)(2,1)S(1)}, bf16[128,512]{1,0:T(8,128)(2,1)}, u32[]{:S(2)}) copy-start(bf16[128,512]{1,0:T(8,128)(2,1)} %param.16) | copy-start | bytes 393220
  11.9 23.6 %copy-start.1 = (bf16[256,1024]{1,0:T(8,128)(2,1)S(1)}, bf16[256,1024]{1,0:T(8,128)(2,1)}, u32[]{:S(2)}) copy-start(bf16[256,1024]{1,0:T(8,128)(2,1)} %param.11) | copy-start | bytes 1572868
  12.0 25.2 %collective-permute-start = (bf16[256,512]{0,1:T(8,128)(2,1)S(1)}, bf16[256,512]{0,1:T(8,128)(2,1)}, u32[]{:S(2)}, u32[]{:S(2)}) collective-permute-start(bf16[256,512]{0,1:T(8,128)(2,1)S(1)} %pad_maximum_fusion.1), channel_id=1, source_target_pairs={{0,4},{4,8},{8,12},{12,16},{16,20},{20,24},{24,28},{28,32},{32,36}... | collective-permute-start | bytes 786440 | tf_op jit(solution)/shard_map/ppermute | solution.py:19
  17.0 20.2 %collective-permute-start.1 = (bf16[256,512]{0,1:T(8,128)(2,1)S(1)}, bf16[256,512]{0,1:T(8,128)(2,1)}, u32[]{:S(2)}, u32[]{:S(2)}) collective-permute-start(bf16[256,512]{0,1:T(8,128)(2,1)S(1)} %pad_maximum_fusion.1), channel_id=1, source_target_pairs={{4,0},{8,4},{12,8},{16,12},{20,16},{24,20},{28,24},{32,28},{36,32}... | collective-permute-start | bytes 786440 | tf_op jit(solution)/shard_map/ppermute | solution.py:21
  19.2 16.5 %copy-start.5 = (f32[1024]{0:T(1024)S(1)}, f32[1024]{0:T(1024)}, u32[]{:S(2)}) copy-start(f32[1024]{0:T(1024)} %param.12) | copy-start | bytes 12292
  35.1 381.2 %all-gather.5.cloned.1.call-start = ((), (), s32[]{:S(2)}) async-start(), calls=%async_computation | async-start | bytes 1052672 | tf_op jit(solution)/shard_map/all_gather | solution.py:110
  40.1 1.6 copy-start.2
  40.1 4.1 copy-start.4
Sparse Core Ops, SparseCore 0:
  35.2 261.0 all-reduce.3
  300.6 103.6 all-gather.4
where the time goes:
time: 624 us; the launch traced here: 622 us
  blocking collectives  311 us (50%)
  waiting for transfers between devices  252 us (40%)
  between operations  15 us (2%)
  local copies, waits for them, and re-layouts  13.2 us (2%)
  matrix products  12.3 us (2%)
  other arithmetic  11 us (2%)
  starting transfers between devices  7.3 us (1%)
    unnamed x3, waiting for transfers between devices  252 us
    all_gather x1, blocking collectives, local(): lax.all_gather(caption_own, ('seq', 'head'), axis=0, tiled=True)  118 us
    all_gather x1, blocking collectives, local(): lax.all_gather(interval_embedding_rows, ('seq', 'head'), axis=0, tiled=True)  117 us
    unnamed x1, blocking collectives  75.9 us
  transfers between devices with their start and end apart: 4, of which 1 were waited for; matrix products, arithmetic and copies ran while one was open for 4% of the time, Pallas kernels for 0%

commit v1 on v0

--- a/solution.py
+++ b/solution.py
@@ -138,7 +138,15 @@
     )
     caption_own = unit_rows(raw).astype(jnp.bfloat16)
     spans_all, captions_all = (
-        lax.all_gather(interval_embedding_rows, ("seq", "head"), axis=0, tiled=True),
+        jnp.concatenate(
+            lax.all_to_all(
+                jnp.stack([interval_embedding_rows] * lax.axis_size(("seq", "head"))),
+                ("seq", "head"),
+                0,
+                0,
+            ),
+            axis=0,
+        ),
         lax.all_gather(caption_own, ("seq", "head"), axis=0, tiled=True),
     )
     normalizer_divisor = contrast_divisor[0]

time: 624 us -> 608 us (0.974)
  blocking collectives: 311 us -> 194 us
  waiting for transfers between devices: 252 us -> 342 us
  starting transfers between devices: 7.3 us -> 17.7 us
    all_gather x1 -> x0, blocking collectives: 117 us -> none  [local(): lax.all_gather(interval_embedding_rows, ('seq', 'head'), axis=0, tiled=True)]
    all_gather x1, waiting for transfers between devices: 0.02 us -> 88.9 us  [local(): lax.all_gather(partial_value, ('seq', 'head'), axis=0, tiled=True)]
    all_to_all x0 -> x1, starting transfers between devices: none -> 10.5 us  [local(): lax.all_to_all(jnp.stack([interval_embedding_rows] * lax.axis_size(('seq'...]
  transfers between devices with their start and end apart: 4 -> 5, of which waited for: 1 -> 3; matrix products, arithmetic and copies ran while one was open for 4% -> 4% of each run, Pallas kernels for 0% -> 0%
where the time goes in v1:
time: 608 us; the launch traced here: 606 us
  waiting for transfers between devices  342 us (56%)
  blocking collectives  194 us (32%)
  starting transfers between devices  17.7 us (3%)
  between operations  15 us (2%)
  local copies, waits for them, and re-layouts  14.2 us (2%)
  matrix products  12.2 us (2%)
  other arithmetic  11.7 us (2%)
    unnamed x3, waiting for transfers between devices  249 us
    all_gather x1, blocking collectives, local(): lax.all_gather(caption_own, ('seq', 'head'), axis=0, tiled=True)  118 us
    all_gather x1, waiting for transfers between devices, local(): lax.all_gather(partial_value, ('seq', 'head'), axis=0, tiled=True)  88.9 us
    unnamed x1, blocking collectives  75.6 us
  transfers between devices with their start and end apart: 5, of which 3 were waited for; matrix products, arithmetic and copies ran while one was open for 4% of the time, Pallas kernels for 0%

profile of v1, /device:TPU:1, one launch (start us, length us, event | category | flops | bytes accessed | tf_op | source)
XLA Modules:
  0.0 606.4 jit_solution(1245762500219217627)
XLA Ops:
  7.2 1.3 multiply_reduce_fusion
  8.6 1.7 convolution_convert_fusion.1
  10.3 1.7 convolution_convert_fusion.2
  12.7 4.9 collective-permute-start
  17.6 2.2 collective-permute-start.1
  20.3 1.5 convolution_convert_fusion
  21.8 3.8 collective-permute-done.1
  25.6 1.1 pad_maximum_fusion
  26.7 0.8 fusion.2
  27.5 0.9 fusion.3
  28.5 1.0 fusion.18
  30.9 0.8 fusion.11
  31.8 14.5 %while.18 = (s32[]{:T(128)}, f32[512,128]{1,0:T(8,128)S(1)}, s32[512,16]{0,1:T(8,128)}, s32[]{:T(128)}, s32[]{:T(128)}, /*index=5*/s32[]{:T(128)}) while((s32[]{:T(128)}, f32[512,128]{1,0:T(8,128)S(1)}, s32[512,16]{0,1:T(8,128)}, s32[]{:T(128)}, s32[]{:T(128)}, /*index=5*/s32[]{:T(128)}) %tuple.47), condition=%wide.region_1.2_spmd.clone, body=%wide.region_0.0_spmd.clone.sunk | while | flops 262275 | bytes 531543 | solution.py:44
  31.8 0.7 constant_dynamic-slice_fusion.4
  32.7 0.7 constant_dynamic-slice_fusion.4
  33.6 0.7 constant_dynamic-slice_fusion.4
  34.5 0.7 constant_dynamic-slice_fusion.4
  35.4 0.7 constant_dynamic-slice_fusion.4
  40.9 0.7 constant_dynamic-slice_fusion.4
  42.7 0.7 constant_dynamic-slice_fusion.4
  46.3 1.3 fusion.30
  48.6 88.9 %all-gather.4.cloned.1.call-done = f32[256,2,512]{2,1,0:T(2,128)} async-done(((f32[1,2,512]{2,1,0:T(2,128)}), f32[256,2,512]{2,1,0:T(2,128)}) %all-gather.4.cloned.1.call-update) | async-done | bytes 1048592 | tf_op jit(solution)/shard_map/all_gather | solution.py:110
  137.5 1.8 bitcast_reduce_fusion
  139.9 1.1 stack.2
  141.0 10.5 %all-to-all-start = ((bf16[256,2,512]{2,1,0:T(2,128)(2,1)}), bf16[256,2,512]{2,1,0:T(2,128)(2,1)S(1)}, u32[]{:S(2)}, u32[]{:S(2)}) async-start(bf16[256,2,512]{2,1,0:T(2,128)(2,1)} %stack.2), calls=%async_computation | async-start | bytes 1048576 | tf_op jit(solution)/shard_map/all_to_all | solution.py:142
  151.6 248.9 %all-reduce.4.cloned.1.call-done = f32[512,512]{1,0:T(8,128)} async-done(((f32[512,512]{1,0:T(8,128)}), f32[512,512]{1,0:T(8,128)}) %all-reduce.4.cloned.1.call-update) | async-done | bytes 1048592
  400.4 0.8 multiply_reduce_fusion.2
  401.3 0.8 fusion.73
  402.1 118.0 %all-gather = bf16[256,2,512]{2,1,0:T(2,128)(2,1)S(1)} all-gather(bf16[1,2,512]{2,1,0:T(2,128)(2,1)S(1)} %fusion.73), channel_id=1, replica_groups=mesh['seq'=64,'head'=4] {'seq','head'}, dimensions={0}, use_global_device_ids=true | all-gather | bytes 526336 | tf_op jit(solution)/shard_map/all_gather | solution.py:150
  520.8 1.1 exponential_reduce_fusion.1
  523.2 75.6 %all-reduce = f32[512]{0:T(512)S(1)} all-reduce(f32[512]{0:T(512)S(1)} %get-tuple-element.129), channel_id=1, replica_groups=mesh['seq'=64,'head'=4] {'seq','head'}, use_global_device_ids=true, to_apply=%add | all-reduce | flops 512 | bytes 4096
  598.8 0.8 convolution_multiply_fusion
  (88 shorter events, 14.7 us)
Async XLA Ops:
  7.2 23.2 %copy-start = (bf16[1024,512]{1,0:T(8,128)(2,1)S(1)}, bf16[1024,512]{1,0:T(8,128)(2,1)}, u32[]{:S(2)}) copy-start(bf16[1024,512]{1,0:T(8,128)(2,1)} %param.15) | copy-start | bytes 3145732
  7.2 12.9 %copy-start.1 = (bf16[256,1024]{1,0:T(8,128)(2,1)S(1)}, bf16[256,1024]{1,0:T(8,128)(2,1)}, u32[]{:S(2)}) copy-start(bf16[256,1024]{1,0:T(8,128)(2,1)} %param.11) | copy-start | bytes 1572868
  7.2 130.4 %all-gather.4.cloned.1.call-start = ((), (), s32[]{:S(2)}) async-start(), calls=%async_computation.1 | async-start | bytes 1052672 | tf_op jit(solution)/shard_map/all_gather | solution.py:110
  8.6 11.7 %copy-start.5 = (f32[1024]{0:T(1024)S(1)}, f32[1024]{0:T(1024)}, u32[]{:S(2)}) copy-start(f32[1024]{0:T(1024)} %param.12) | copy-start | bytes 12292
  12.7 9.2 %collective-permute-start = (bf16[256,512]{0,1:T(8,128)(2,1)}, bf16[256,512]{0,1:T(8,128)(2,1)}, u32[]{:S(2)}, u32[]{:S(2)}) collective-permute-start(bf16[256,512]{0,1:T(8,128)(2,1)} %pad_maximum_fusion.1), channel_id=1, source_target_pairs={{0,4},{4,8},{8,12},{12,16},{16,20},{20,24},{24,28},{28,32},{32,36}... | collective-permute-start | bytes 786440 | tf_op jit(solution)/shard_map/ppermute | solution.py:19
  17.6 8.0 %collective-permute-start.1 = (bf16[256,512]{0,1:T(8,128)(2,1)}, bf16[256,512]{0,1:T(8,128)(2,1)}, u32[]{:S(2)}, u32[]{:S(2)}) collective-permute-start(bf16[256,512]{0,1:T(8,128)(2,1)} %pad_maximum_fusion.1), channel_id=1, source_target_pairs={{4,0},{8,4},{12,8},{16,12},{20,16},{24,20},{28,24},{32,28},{36,32}... | collective-permute-start | bytes 786440 | tf_op jit(solution)/shard_map/ppermute | solution.py:21
  28.5 1.5 copy-start.2
  29.5 16.8 %copy-start.3 = (bf16[128,512]{1,0:T(8,128)(2,1)S(1)}, bf16[128,512]{1,0:T(8,128)(2,1)}, u32[]{:S(2)}) copy-start(bf16[128,512]{1,0:T(8,128)(2,1)} %param.16) | copy-start | bytes 393220
  30.4 17.4 %copy-start.4 = (s32[2,2]{1,0:T(2,128)S(1)}, s32[2,2]{1,0:T(2,128)}, u32[]{:S(2)}) copy-start(s32[2,2]{1,0:T(2,128)} %param.18) | copy-start | bytes 52
  31.7 368.7 %all-reduce.4.cloned.1.call-start = ((), (), s32[]{:S(2)}) async-start(), calls=%async_computation.2 | async-start | bytes 2097152
  141.0 379.6 %all-to-all-start = ((bf16[256,2,512]{2,1,0:T(2,128)(2,1)}), bf16[256,2,512]{2,1,0:T(2,128)(2,1)S(1)}, u32[]{:S(2)}, u32[]{:S(2)}) async-start(bf16[256,2,512]{2,1,0:T(2,128)(2,1)} %stack.2), calls=%async_computation | async-start | bytes 1048576 | tf_op jit(solution)/shard_map/all_to_all | solution.py:142
Sparse Core Ops, SparseCore 0:
  31.9 105.6 all-gather.3
  143.0 257.4 all-reduce.3
